TPU v7x, 256 devices: a whole 4x4x8 slice. The times are simulated.
256 devices in a mesh: dp: 8 (over y, core), proto: 32 (over z, x).
Axes of the slice: x: 4, y: 4, z: 8, core: 2. Of those that a mesh axis runs over, the one named last changes fastest.
Arguments:
- teacher_features: bfloat16 [6144, 384], P('dp'), may hold values from -8 to 8
- student_features: bfloat16 [6144, 384], P('dp'), may hold values from -8 to 8
- teacher_weight: bfloat16 [384, 131072], P('dp', 'proto'), may hold values from -1 to 1
- student_weight: bfloat16 [384, 131072], P('dp', 'proto'), may hold values from -1 to 1
Outputs:
- teacher_codes: bfloat16 [6144, 131072], P('dp', 'proto')
- head_loss: float32 [], replicated
- weight_grad: float32 [384, 131072], P('dp', 'proto')
All inputs are finite; a program needn't handle non-finite values.
Results may differ from a plain program's by a relative error of at most 0.003.
Values may be sent and summed in bfloat16 or wider, within the bound.
A program may use at most 128 MiB of HBM per device.

v0:
```python
import jax
import jax.numpy as jnp
from jax import lax
from jax.sharding import PartitionSpec as P

ITERS = 3
teacher_temp = 0.07
student_temp = 0.1
norm_eps = 1e-06


def column_norm(weight_rows):
    return jnp.sqrt(jnp.sum(jnp.square(weight_rows.astype(jnp.float32)), axis=0) + norm_eps)


def body(teacher_features, student_features, teacher_weight, student_weight):
    local_crops = teacher_features.shape[0]
    total_crops = local_crops * lax.axis_size("dp")
    total_protos = teacher_weight.shape[1] * lax.axis_size("proto")
    teacher_full, student_full = (
        lax.all_gather(teacher_weight, "dp", axis=0, tiled=True),
        lax.all_gather(student_weight, "dp", axis=0, tiled=True),
    )
    teacher_norm = column_norm(teacher_full)
    student_norm = column_norm(student_full)
    teacher_logits = (
        jnp.dot(teacher_features, teacher_full, preferred_element_type=jnp.float32) / teacher_norm
    )
    student_logits = (
        jnp.dot(student_features, student_full, preferred_element_type=jnp.float32) / student_norm
    )
    teacher_peak, student_peak = lax.pmax(
        (jnp.max(teacher_logits, axis=1), jnp.max(student_logits, axis=1)), "proto"
    )
    powers = jnp.exp((teacher_logits - teacher_peak[:, None]) / teacher_temp)
    shifted = (student_logits - student_peak[:, None]) / student_temp
    student_local = jnp.sum(jnp.exp(shifted), axis=1)
    crop_scale = jnp.ones((local_crops,), jnp.float32)
    for sweep_index in range(ITERS):
        proto_mass = lax.psum(jnp.dot(crop_scale, powers, precision=lax.Precision.HIGHEST), "dp")
        proto_scale = 1.0 / (total_protos * proto_mass)
        crop_local = jnp.dot(powers, proto_scale, precision=lax.Precision.HIGHEST)
        if sweep_index == 0:
            crop_mass = lax.psum(crop_local, "proto")
        else:
            crop_mass = lax.psum(crop_local, "proto")
        crop_scale = 1.0 / (total_crops * crop_mass)
    student_total = lax.psum(student_local, "proto")
    assign = powers * proto_scale[None, :] * crop_scale[:, None] * total_crops
    teacher_codes = assign.astype(jnp.bfloat16)
    log_prob = shifted - jnp.log(student_total)[:, None]
    loss_local = -jnp.sum(assign * log_prob)
    signal = ((jnp.exp(log_prob) - assign) / student_temp).astype(jnp.bfloat16)
    head_loss = lax.psum(loss_local, ("dp", "proto")) / total_crops
    own_weight = student_weight.astype(jnp.float32) / student_norm
    own_grad = lax.psum_scatter(
        lax.dot_general(
            student_features, signal, (((0,), (0,)), ((), ())), preferred_element_type=jnp.float32
        ),
        "dp",
        scatter_dimension=0,
        tiled=True,
    )
    pressure = lax.psum(jnp.sum(own_grad * own_weight, axis=0), "dp")
    weight_grad = (own_grad - own_weight * pressure[None, :]) / student_norm
    return (teacher_codes, head_loss, weight_grad)


def solution(mesh):
    return jax.shard_map(
        body,
        mesh=mesh,
        in_specs=(P("dp", None), P("dp", None), P("dp", "proto"), P("dp", "proto")),
        out_specs=(P("dp", "proto"), P(), P("dp", "proto")),
        check_vma=False,
    )
```

profile of v0, /device:TPU:32, one launch (start us, length us, event | category | flops | bytes accessed | tf_op | source)
XLA Modules:
  0.0 684.9 jit_solution(6292353373318271310)
XLA Ops:
  7.2 0.0 copy-start
  7.2 0.0 all-gather.5.cloned.1.call-start
  7.2 0.7 all-gather.5.cloned.1.call-update
  7.9 0.0 all-gather.3.cloned.1.call-start
  8.0 0.7 all-gather.3.cloned.1.call-update
  8.7 0.0 reduce-scatter.4.cloned.1.call-start
  8.7 34.1 %all-gather.5.cloned.1.call-done = bf16[384,4096]{1,0:T(8,128)(2,1)} async-done(((bf16[48,4096]{1,0:T(8,128)(2,1)}), bf16[384,4096]{1,0:T(8,128)(2,1)}) %all-gather.5.cloned.1.call-update) | async-done | bytes 3145744 | tf_op jit(solution)/shard_map/all_gather | solution.py:22
  42.8 2.6 multiply_reduce_fusion.1
  45.4 29.6 %all-gather.3.cloned.1.call-done = bf16[384,4096]{1,0:T(8,128)(2,1)} async-done(((bf16[48,4096]{1,0:T(8,128)(2,1)}), bf16[384,4096]{1,0:T(8,128)(2,1)}) %all-gather.3.cloned.1.call-update) | async-done | bytes 3145744 | tf_op jit(solution)/shard_map/all_gather | solution.py:21
  75.1 2.6 multiply_reduce_fusion.2
  77.6 0.0 copy-done
  77.7 0.0 copy-start.2
  77.7 0.0 copy-start.4
  77.7 8.5 %fusion.9 = (f32[768]{0:T(1024)S(1)}, f32[768,4096]{1,0:T(8,128)}) fusion(f32[4096]{0:T(1024)S(1)} %add_sqrt_fusion, bf16[768,384]{1,0:T(8,128)(2,1)S(1)} %copy-done, bf16[384,4096]{1,0:T(8,128)(2,1)} %all-gather.5.cloned.1.call-done), kind=kOutput, calls=%fused_computation.33 | convolution fusion | flops 2422209792 | bytes 16337920 | tf_op jit(solution)/shard_map/dot_general | solution.py:30
  86.2 0.0 copy-done.2
  86.2 0.0 copy-done.4
  86.2 6.4 fusion.3
  92.6 70.3 %all-reduce.1 = (f32[768]{0:T(1024)S(1)}, f32[768]{0:T(1024)S(1)}) all-reduce(f32[768]{0:T(1024)S(1)} %get-tuple-element.15, f32[768]{0:T(1024)S(1)} %get-tuple-element.17), channel_id=1, replica_groups=mesh['dp'=8,'proto'=32] {'proto'}, use_global_device_ids=true, to_apply=%region_2.0 | all-reduce | flops 1536 | bytes 12288 | tf_op jit(solution)/shard_map/pmax | solution.py:32
  162.9 10.4 %exponential_reduce_fusion = (f32[768]{0:T(1024)S(1)}, f32[768,4096]{1,0:T(8,128)S(1)}) fusion(f32[768,4096]{1,0:T(8,128)} %get-tuple-element.18, f32[768]{0:T(1024)S(1)} %get-tuple-element.12, f32[768]{0:T(1024)S(1)} %get-tuple-element.11, f32[768,4096]{1,0:T(8,128)} %get-tuple-element.16, f32[4096]{0:T(1024)S(1)} %add_sqrt_fusion.1), kind=kLoop, calls=%fused_computation.2 | loop fusion | flops 18873600 | bytes 37774336 | tf_op jit(solution)/shard_map/reduce_sum | solution.py:37
  173.4 0.0 copy-start.1
  173.4 4.5 copy-done.1
  177.8 6.0 fusion.4
  183.8 24.1 %psum.63 = f32[4096]{0:T(1024)S(1)} all-reduce(f32[4096]{0:T(1024)S(1)} %bitcast.30), channel_id=1, replica_groups=mesh['dp'=8,'proto'=32] {'dp'}, use_global_device_ids=true, to_apply=%region_3.0 | all-reduce | flops 4096 | bytes 32768 | tf_op jit(solution)/shard_map/psum | solution.py:40
  207.9 13.3 %convolution_reduce_fusion.2 = f32[768]{0:T(1024)S(1)} fusion(f32[768,4096]{1,0:T(8,128)} %copy-done.1, f32[4096,1]{0,1:T(1,128)S(1)} %bitcast.26), kind=kOutput, calls=%fused_computation.19 | convolution fusion | flops 37748736 | bytes 12602368 | tf_op jit(solution)/shard_map/dot_general | solution.py:42
  221.2 69.6 %psum.64 = f32[768]{0:T(1024)S(1)} all-reduce(f32[768]{0:T(1024)S(1)} %convolution_reduce_fusion.2), channel_id=1, replica_groups=mesh['dp'=8,'proto'=32] {'proto'}, use_global_device_ids=true, to_apply=%region_4.0 | all-reduce | flops 768 | bytes 6144 | tf_op jit(solution)/shard_map/psum | solution.py:44
  290.9 8.5 %fusion.10 = f32[1,4096]{1,0:T(1,128)S(1)} fusion(f32[768,1]{0,1:T(1,128)S(1)} %reshape.24, f32[768,4096]{1,0:T(8,128)} %copy-done.1), kind=kOutput, calls=%fused_computation.34 | convolution fusion | flops 37748736 | bytes 12602368 | tf_op jit(solution)/shard_map/dot_general | solution.py:40
  299.4 23.6 %psum.65 = f32[4096]{0:T(1024)S(1)} all-reduce(f32[4096]{0:T(1024)S(1)} %bitcast.27), channel_id=1, replica_groups=mesh['dp'=8,'proto'=32] {'dp'}, use_global_device_ids=true, to_apply=%region_5.0 | all-reduce | flops 4096 | bytes 32768 | tf_op jit(solution)/shard_map/psum | solution.py:40
  323.0 13.3 %convolution_reduce_fusion.1 = f32[768]{0:T(1024)S(1)} fusion(f32[768,4096]{1,0:T(8,128)} %copy-done.1, f32[4096,1]{0,1:T(1,128)S(1)} %bitcast.28), kind=kOutput, calls=%fused_computation.18 | convolution fusion | flops 37748736 | bytes 12602368 | tf_op jit(solution)/shard_map/dot_general | solution.py:42
  336.3 71.8 %psum.66 = f32[768]{0:T(1024)S(1)} all-reduce(f32[768]{0:T(1024)S(1)} %convolution_reduce_fusion.1), channel_id=1, replica_groups=mesh['dp'=8,'proto'=32] {'proto'}, use_global_device_ids=true, to_apply=%region_6.0 | all-reduce | flops 768 | bytes 6144 | tf_op jit(solution)/shard_map/psum | solution.py:46
  408.1 8.5 %fusion.11 = f32[1,4096]{1,0:T(1,128)S(1)} fusion(f32[768,1]{0,1:T(1,128)S(1)} %reshape.28, f32[768,4096]{1,0:T(8,128)} %copy-done.1), kind=kOutput, calls=%fused_computation.35 | convolution fusion | flops 37748736 | bytes 12602368 | tf_op jit(solution)/shard_map/dot_general | solution.py:40
  416.6 23.6 %psum.67 = f32[4096]{0:T(1024)S(1)} all-reduce(f32[4096]{0:T(1024)S(1)} %bitcast.29), channel_id=1, replica_groups=mesh['dp'=8,'proto'=32] {'dp'}, use_global_device_ids=true, to_apply=%region_7.0 | all-reduce | flops 4096 | bytes 32768 | tf_op jit(solution)/shard_map/psum | solution.py:40
  440.2 13.3 %convolution_reduce_fusion = f32[768]{0:T(1024)S(1)} fusion(f32[768,4096]{1,0:T(8,128)} %copy-done.1, f32[4096,1]{0,1:T(1,128)S(1)} %bitcast.25), kind=kOutput, calls=%fused_computation.17 | convolution fusion | flops 37748736 | bytes 12602368 | tf_op jit(solution)/shard_map/dot_general | solution.py:42
  453.5 70.9 %all-reduce = (f32[768]{0:T(1024)S(1)}, f32[768]{0:T(1024)S(1)}) all-reduce(f32[768]{0:T(1024)S(1)} %convolution_reduce_fusion, f32[768]{0:T(1024)S(1)} %get-tuple-element.19), channel_id=1, replica_groups=mesh['dp'=8,'proto'=32] {'proto'}, use_global_device_ids=true, to_apply=%region_8.0 | all-reduce | flops 1536 | bytes 12288 | tf_op jit(solution)/shard_map/psum | solution.py:46
  524.4 13.1 %fusion.2 = f32[384,4096]{0,1:T(8,128)} fusion(bf16[768,384]{1,0:T(8,128)(2,1)S(1)} %copy-done, f32[768,4096]{1,0:T(8,128)} %get-tuple-element.18, f32[768,4096]{1,0:T(8,128)} %copy-done.1, f32[768]{0:T(1024)S(1)} %log.3, f32[768]{0:T(1024)S(1)} %get-tuple-element.12, f32[768]{0:T(1024)S(1)} %multiply_divide_fusion.3, f32[4096]{0:T(1024)S(1)} %multiply_divide_fusion), kind=kOutput, calls=%fused_computation.12 | convolution fusion | flops 2444230656 | bytes 32072704 | tf_op jit(solution)/shard_map/dot_general | solution.py:57
  537.5 6.5 copy.11
  544.0 0.0 reduce-scatter.4.cloned.1.call-update
  544.0 0.0 copy-start.3
  544.0 14.4 %multiply_reduce_fusion = (f32[]{:T(128)}, bf16[768,4096]{1,0:T(8,128)(2,1)}) fusion(f32[768,4096]{1,0:T(8,128)} %get-tuple-element.18, f32[768,4096]{1,0:T(8,128)} %copy-done.1, f32[768]{0:T(1024)S(1)} %log.3, f32[768]{0:T(1024)S(1)} %get-tuple-element.12, f32[768]{0:T(1024)S(1)} %multiply_divide_fusion.3, f32[4096]{0:T(1024)S(1)} %multiply_divide_fusion), kind=kLoop, calls=%fused_computation.1 | loop fusion | flops 28311552 | bytes 31482884 | tf_op jit(solution)/shard_map/reduce_sum | solution.py:52
  559.1 0.0 copy-done.3
  559.1 1.3 copy.9
  560.4 80.6 %psum.70 = f32[]{:T(128)} all-reduce(f32[]{:T(128)S(6)} %neg.3), channel_id=1, replica_groups=mesh['dp'=8,'proto'=32] {'dp','proto'}, use_global_device_ids=true, to_apply=%region_15.0 | all-reduce | flops 1 | bytes 8 | tf_op jit(solution)/shard_map/psum | solution.py:54
  641.7 0.0 reduce-scatter.4.cloned.1.call-done
  641.7 1.7 copy.12
  643.4 2.3 multiply_reduce_fusion.3
  645.8 23.6 %psum.71 = f32[4096]{0:T(1024)S(1)} all-reduce(f32[4096]{0:T(1024)S(1)} %multiply_reduce_fusion.3), channel_id=1, replica_groups=mesh['dp'=8,'proto'=32] {'dp'}, use_global_device_ids=true, to_apply=%region_18.0 | all-reduce | flops 4096 | bytes 32768 | tf_op jit(solution)/shard_map/psum | solution.py:64
  669.3 4.6 subtract_divide_fusion
  673.9 3.1 copy.10
  (11 shorter events, 0.1 us)
Async XLA Ops:
  7.2 70.5 %copy-start = (bf16[768,384]{1,0:T(8,128)(2,1)S(1)}, bf16[768,384]{1,0:T(8,128)(2,1)}, u32[]{:S(2)}) copy-start(bf16[768,384]{1,0:T(8,128)(2,1)} %param.5) | copy-start | bytes 1769476
  7.2 35.6 %all-gather.5.cloned.1.call-start = ((), (), s32[]{:S(2)}) async-start(), calls=%async_computation.2 | async-start | bytes 3538944 | tf_op jit(solution)/shard_map/all_gather | solution.py:22
  7.9 67.1 %all-gather.3.cloned.1.call-start = ((), (), s32[]{:S(2)}) async-start(), calls=%async_computation.1 | async-start | bytes 3538944 | tf_op jit(solution)/shard_map/all_gather | solution.py:21
  8.7 633.0 %reduce-scatter.4.cloned.1.call-start = ((), (), s32[]{:S(2)}) async-start(), calls=%async_computation.3 | async-start | bytes 7077888
  77.7 8.6 %copy-start.2 = (bf16[384,4096]{1,0:T(8,128)(2,1)S(1)}, bf16[384,4096]{1,0:T(8,128)(2,1)}, u32[]{:S(2)}) copy-start(bf16[384,4096]{1,0:T(8,128)(2,1)} %all-gather.3.cloned.1.call-done) | copy-start | bytes 9437188
  77.7 8.6 %copy-start.4 = (bf16[768,384]{1,0:T(8,128)(2,1)S(1)}, bf16[768,384]{1,0:T(8,128)(2,1)}, u32[]{:S(2)}) copy-start(bf16[768,384]{1,0:T(8,128)(2,1)} %param.4) | copy-start | bytes 1769476
  173.4 4.5 copy-start.1
  544.0 15.1 %copy-start.3 = (bf16[48,4096]{1,0:T(8,128)(2,1)S(1)}, bf16[48,4096]{1,0:T(8,128)(2,1)}, u32[]{:S(2)}) copy-start(bf16[48,4096]{1,0:T(8,128)(2,1)} %param.7) | copy-start | bytes 1179652
Sparse Core Ops, SparseCore 0:
  9.8 32.9 all-gather.4
  44.6 30.3 all-gather.2
  544.2 46.9 reduce-scatter.3
where the time goes:
time: 689 us; the launch traced here: 685 us
  blocking collectives  458 us (66%)
  matrix products  91 us (13%)
  waiting for transfers between devices  65.2 us (9%)
  other arithmetic  37 us (5%)
  local copies, waits for them, and re-layouts  17.1 us (2%)
  between operations  16.6 us (2%)
    psum x3, blocking collectives, body(): crop_mass = lax.psum(crop_local, 'proto')  212 us
    psum x1, blocking collectives, body(): head_loss = lax.psum(loss_local, ('dp', 'proto')) / total_crops  80.6 us
    psum x3, blocking collectives, body(): lax.psum(jnp.dot(crop_scale, powers, precision=lax.Precision.HIGHEST), 'dp')  71.2 us
    pmax x1, blocking collectives, body(): lax.pmax((jnp.max(teacher_logits, axis=1), jnp.max(student_logits, axis=1...  70.3 us
    dot_general x3, matrix products, body(): crop_local = jnp.dot(powers, proto_scale, precision=lax.Precision.HIGHEST)  39.9 us
    all_gather x1, waiting for transfers between devices, body(): lax.all_gather(student_weight, 'dp', axis=0, tiled=True)  34.1 us
    all_gather x1, waiting for transfers between devices, body(): lax.all_gather(teacher_weight, 'dp', axis=0, tiled=True)  29.6 us
    psum x1, blocking collectives, body(): pressure = lax.psum(jnp.sum(own_grad * own_weight, axis=0), 'dp')  23.6 us
  transfers between devices with their start and end apart: 3, of which 2 were waited for; matrix products, arithmetic and copies ran while one was open for 3% of the time, Pallas kernels for 0%

commit v1 on v0

--- a/solution.py
+++ b/solution.py
@@ -2,11 +2,38 @@
 import jax.numpy as jnp
 from jax import lax
 from jax.sharding import PartitionSpec as P
+from jax.lax import axis_index, axis_size, ppermute
 
 ITERS = 3
 teacher_temp = 0.07
 student_temp = 0.1
 norm_eps = 1e-06
+
+
+def remake_arrays_over_axis(message):
+    total_devices = axis_size("dp")
+    slots = []
+    hop_no = 0
+    while hop_no < total_devices:
+        slots.append((hop_no, (hop_no + 1) % total_devices))
+        hop_no = hop_no + 1
+    rack = []
+    hop_no = 0
+    while hop_no < total_devices:
+        rack.append((hop_no, (hop_no - 1) % total_devices))
+        hop_no += 1
+    val2, n_now = ([message], [message])
+    for _ in range(total_devices // 2):
+        now = ppermute(val2[-1], "dp", slots)
+        val2.append(now)
+    dev = 0
+    while dev < (total_devices - 1) // 2:
+        m_next = ppermute(n_now[-1], "dp", rack)
+        n_now.append(m_next)
+        dev += 1
+    found_now = jnp.concatenate([*val2[::-1], *n_now[1:]], 0)
+    carry = axis_index("dp")
+    return jnp.roll(found_now, (carry - total_devices // 2) * message.shape[0], 0)
 
 
 def column_norm(weight_rows):
@@ -19,7 +46,7 @@
     total_protos = teacher_weight.shape[1] * lax.axis_size("proto")
     teacher_full, student_full = (
         lax.all_gather(teacher_weight, "dp", axis=0, tiled=True),
-        lax.all_gather(student_weight, "dp", axis=0, tiled=True),
+        remake_arrays_over_axis(student_weight),
     )
     teacher_norm = column_norm(teacher_full)
     student_norm = column_norm(student_full)

time: 689 us -> 674 us (0.978)
  waiting for transfers between devices: 65.2 us -> 40 us
  starting transfers between devices: 0.11 us -> 9.13 us
    all_gather x1 -> x0, waiting for transfers between devices: 34.1 us -> none  [body(): lax.all_gather(student_weight, 'dp', axis=0, tiled=True)]
    ppermute x0 -> x7, waiting for transfers between devices: none -> 24.7 us  [the longest x4 24.6 us: remake_arrays_over_axis(): now = ppermute(val2[-1], 'dp', slots)]
    all_gather x1, waiting for transfers between devices: 29.6 us -> 15.2 us  [body(): lax.all_gather(teacher_weight, 'dp', axis=0, tiled=True)]
    ppermute x0 -> x7, starting transfers between devices: none -> 9.05 us  [the longest x3 9.02 us: remake_arrays_over_axis(): m_next = ppermute(n_now[-1], 'dp', rack)]
    unnamed x14 -> x27, local copies, waits for them, and re-layouts: 17.1 us -> 14.1 us
  transfers between devices with their start and end apart: 3 -> 9, of which waited for: 2 -> 6; matrix products, arithmetic and copies ran while one was open for 3% -> 4% of each run, Pallas kernels for 0% -> 0%
where the time goes in v1:
time: 674 us; the launch traced here: 668 us
  blocking collectives  458 us (68%)
  matrix products  90.9 us (13%)
  waiting for transfers between devices  40 us (6%)
  other arithmetic  39.2 us (6%)
  between operations  17.1 us (3%)
  local copies, waits for them, and re-layouts  14.1 us (2%)
  starting transfers between devices  9.13 us (1%)
    psum x3, blocking collectives, body(): crop_mass = lax.psum(crop_local, 'proto')  212 us
    psum x1, blocking collectives, body(): head_loss = lax.psum(loss_local, ('dp', 'proto')) / total_crops  80.6 us
    psum x3, blocking collectives, body(): lax.psum(jnp.dot(crop_scale, powers, precision=lax.Precision.HIGHEST), 'dp')  70.9 us
    pmax x1, blocking collectives, body(): lax.pmax((jnp.max(teacher_logits, axis=1), jnp.max(student_logits, axis=1...  70.5 us
    dot_general x3, matrix products, body(): crop_local = jnp.dot(powers, proto_scale, precision=lax.Precision.HIGHEST)  39.9 us
    ppermute x4, waiting for transfers between devices, remake_arrays_over_axis(): now = ppermute(val2[-1], 'dp', slots)  24.6 us
    psum x1, blocking collectives, body(): pressure = lax.psum(jnp.sum(own_grad * own_weight, axis=0), 'dp')  23.6 us
    dot_general x3, matrix products, body(): jnp.dot(crop_scale, powers, precision=lax.Precision.HIGHEST)  23 us
  transfers between devices with their start and end apart: 9, of which 6 were waited for; matrix products, arithmetic and copies ran while one was open for 4% of the time, Pallas kernels for 0%

profile of v1, /device:TPU:32, one launch (start us, length us, event | category | flops | bytes accessed | tf_op | source)
XLA Modules:
  0.0 668.2 jit_solution(1558070334485101536)
XLA Ops:
  7.2 0.0 copy-start
  7.2 0.0 copy-start.2
  7.2 0.0 all-gather.2.cloned.1.call-start
  7.2 0.0 collective-permute-start
  7.3 8.6 %collective-permute-done = bf16[48,4096]{1,0:T(8,128)(2,1)S(1)} collective-permute-done((bf16[48,4096]{1,0:T(8,128)(2,1)}, bf16[48,4096]{1,0:T(8,128)(2,1)S(1)}, u32[]{:S(2)}, u32[]{:S(2)}) %collective-permute-start) | collective-permute-done | bytes 393248 | tf_op jit(solution)/shard_map/ppermute | solution.py:27
  15.9 3.0 collective-permute-start.4
  18.8 5.5 collective-permute-done.1
  24.3 0.2 collective-permute-done.4
  24.4 3.0 collective-permute-start.5
  27.5 5.2 collective-permute-done.2
  32.7 0.0 all-gather.2.cloned.1.call-update
  32.7 0.0 reduce-scatter.4.cloned.1.call-start
  32.8 3.1 collective-permute-start.6
  35.9 5.2 collective-permute-done.3
  41.2 1.0 constant_dynamic-update-slice_fusion.11
  42.7 1.1 multiply_reduce_fusion
  43.8 0.0 copy-start.3
  43.8 6.6 fusion.18
  50.4 15.2 %all-gather.2.cloned.1.call-done = bf16[384,4096]{1,0:T(8,128)(2,1)} async-done(((bf16[48,4096]{1,0:T(8,128)(2,1)}), bf16[384,4096]{1,0:T(8,128)(2,1)}) %all-gather.2.cloned.1.call-update) | async-done | bytes 3145744 | tf_op jit(solution)/shard_map/all_gather | solution.py:48
  65.6 2.6 multiply_reduce_fusion.1
  68.2 8.2 %fusion.10 = (f32[768]{0:T(1024)S(1)}, f32[768,4096]{1,0:T(8,128)}) fusion(f32[4096]{0:T(1024)S(1)} %add_sqrt_fusion.1, bf16[768,384]{1,0:T(8,128)(2,1)S(1)} %copy-done.3, bf16[384,4096]{1,0:T(8,128)(2,1)} %all-gather.2.cloned.1.call-done), kind=kOutput, calls=%fused_computation.17 | convolution fusion | flops 2422209792 | bytes 16337920 | tf_op jit(solution)/shard_map/dot_general | solution.py:54
  76.5 70.5 %all-reduce.1 = (f32[768]{0:T(1024)S(1)}, f32[768]{0:T(1024)S(1)}) all-reduce(f32[768]{0:T(1024)S(1)} %get-tuple-element.15, f32[768]{0:T(1024)S(1)} %get-tuple-element.17), channel_id=1, replica_groups=mesh['dp'=8,'proto'=32] {'proto'}, use_global_device_ids=true, to_apply=%region_2.3 | all-reduce | flops 1536 | bytes 12288 | tf_op jit(solution)/shard_map/pmax | solution.py:59
  147.0 6.1 multiply_exponential_fusion
  153.1 6.0 fusion.12
  159.1 23.5 %psum.63 = f32[4096]{0:T(1024)S(1)} all-reduce(f32[4096]{0:T(1024)S(1)} %bitcast.43), channel_id=1, replica_groups=mesh['dp'=8,'proto'=32] {'dp'}, use_global_device_ids=true, to_apply=%region_3.4 | all-reduce | flops 4096 | bytes 32768 | tf_op jit(solution)/shard_map/psum | solution.py:67
  182.6 13.3 %convolution_reduce_fusion.2 = f32[768]{0:T(1024)S(1)} fusion(f32[768,4096]{1,0:T(8,128)} %copy-done.1, f32[4096,1]{0,1:T(1,128)S(1)} %bitcast.39), kind=kOutput, calls=%fused_computation.24 | convolution fusion | flops 37748736 | bytes 12602368 | tf_op jit(solution)/shard_map/dot_general | solution.py:69
  195.9 69.8 %psum.64 = f32[768]{0:T(1024)S(1)} all-reduce(f32[768]{0:T(1024)S(1)} %convolution_reduce_fusion.2), channel_id=1, replica_groups=mesh['dp'=8,'proto'=32] {'proto'}, use_global_device_ids=true, to_apply=%region_4.5 | all-reduce | flops 768 | bytes 6144 | tf_op jit(solution)/shard_map/psum | solution.py:71
  265.8 8.5 %fusion.19 = f32[1,4096]{1,0:T(1,128)S(1)} fusion(f32[768,1]{0,1:T(1,128)S(1)} %reshape.24, f32[768,4096]{1,0:T(8,128)} %copy-done.1), kind=kOutput, calls=%fused_computation.56 | convolution fusion | flops 37748736 | bytes 12602368 | tf_op jit(solution)/shard_map/dot_general | solution.py:67
  274.3 23.6 %psum.65 = f32[4096]{0:T(1024)S(1)} all-reduce(f32[4096]{0:T(1024)S(1)} %bitcast.40), channel_id=1, replica_groups=mesh['dp'=8,'proto'=32] {'dp'}, use_global_device_ids=true, to_apply=%region_5.6 | all-reduce | flops 4096 | bytes 32768 | tf_op jit(solution)/shard_map/psum | solution.py:67
  297.9 13.3 %convolution_reduce_fusion.1 = f32[768]{0:T(1024)S(1)} fusion(f32[768,4096]{1,0:T(8,128)} %copy-done.1, f32[4096,1]{0,1:T(1,128)S(1)} %bitcast.41), kind=kOutput, calls=%fused_computation.23 | convolution fusion | flops 37748736 | bytes 12602368 | tf_op jit(solution)/shard_map/dot_general | solution.py:69
  311.2 71.6 %psum.66 = f32[768]{0:T(1024)S(1)} all-reduce(f32[768]{0:T(1024)S(1)} %convolution_reduce_fusion.1), channel_id=1, replica_groups=mesh['dp'=8,'proto'=32] {'proto'}, use_global_device_ids=true, to_apply=%region_6.7 | all-reduce | flops 768 | bytes 6144 | tf_op jit(solution)/shard_map/psum | solution.py:73
  382.8 8.5 %fusion.20 = f32[1,4096]{1,0:T(1,128)S(1)} fusion(f32[768,1]{0,1:T(1,128)S(1)} %reshape.28, f32[768,4096]{1,0:T(8,128)} %copy-done.1), kind=kOutput, calls=%fused_computation.57 | convolution fusion | flops 37748736 | bytes 12602368 | tf_op jit(solution)/shard_map/dot_general | solution.py:67
  391.4 23.8 %psum.67 = f32[4096]{0:T(1024)S(1)} all-reduce(f32[4096]{0:T(1024)S(1)} %bitcast.42), channel_id=1, replica_groups=mesh['dp'=8,'proto'=32] {'dp'}, use_global_device_ids=true, to_apply=%region_7.8 | all-reduce | flops 4096 | bytes 32768 | tf_op jit(solution)/shard_map/psum | solution.py:67
  415.2 13.3 %convolution_reduce_fusion = f32[768]{0:T(1024)S(1)} fusion(f32[768,4096]{1,0:T(8,128)} %copy-done.1, f32[4096,1]{0,1:T(1,128)S(1)} %bitcast.38), kind=kOutput, calls=%fused_computation.22 | convolution fusion | flops 37748736 | bytes 12602368 | tf_op jit(solution)/shard_map/dot_general | solution.py:69
  428.5 6.7 %exponential_reduce_fusion = f32[768]{0:T(1024)S(1)} fusion(f32[4096,768]{0,1:T(8,128)} %get-tuple-element.18, f32[768]{0:T(1024)S(1)} %get-tuple-element.12), kind=kLoop, calls=%fused_computation.6 | loop fusion | flops 9436416 | bytes 12589056 | tf_op jit(solution)/shard_map/reduce_sum | solution.py:64
  435.2 70.9 %all-reduce = (f32[768]{0:T(1024)S(1)}, f32[768]{0:T(1024)S(1)}) all-reduce(f32[768]{0:T(1024)S(1)} %convolution_reduce_fusion, f32[768]{0:T(1024)S(1)} %exponential_reduce_fusion), channel_id=1, replica_groups=mesh['dp'=8,'proto'=32] {'proto'}, use_global_device_ids=true, to_apply=%region_8.9 | all-reduce | flops 1536 | bytes 12288 | tf_op jit(solution)/shard_map/psum | solution.py:73
  506.1 13.1 %fusion.7 = f32[384,4096]{0,1:T(8,128)} fusion(bf16[768,384]{1,0:T(8,128)(2,1)S(1)} %copy-done, f32[4096,768]{0,1:T(8,128)} %get-tuple-element.18, f32[768,4096]{1,0:T(8,128)} %copy-done.1, f32[768]{0:T(1024)S(1)} %log.3, f32[768]{0:T(1024)S(1)} %get-tuple-element.12, f32[768]{0:T(1024)S(1)} %multiply_divide_fusion.3, f32[4096]{0:T(1024)S(1)} %multiply_divide_fusion), kind=kOutput, calls=%fused_computation.16 | convolution fusion | flops 2444230656 | bytes 32072704 | tf_op jit(solution)/shard_map/dot_general | solution.py:84
  519.2 6.5 copy.14
  525.7 0.0 reduce-scatter.4.cloned.1.call-update
  525.8 15.7 %fusion = (f32[]{:T(128)}, bf16[768,4096]{1,0:T(8,128)(2,1)}) fusion(f32[4096,768]{0,1:T(8,128)} %get-tuple-element.18, f32[768]{0:T(1024)S(1)} %log.3, f32[768]{0:T(1024)S(1)} %get-tuple-element.12, f32[768]{0:T(1024)S(1)} %multiply_divide_fusion.3, f32[4096]{0:T(1024)S(1)} %multiply_divide_fusion, f32[768]{0:T(1024)S(1)} %get-tuple-element.11, ...), kind=kLoop, calls=%fused_computation.2 | loop fusion | flops 37748736 | bytes 31502340 | tf_op jit(solution)/shard_map/reduce_sum | solution.py:79
  542.1 1.3 copy.11
  543.4 80.6 %psum.70 = f32[]{:T(128)} all-reduce(f32[]{:T(128)S(6)} %neg.3), channel_id=1, replica_groups=mesh['dp'=8,'proto'=32] {'dp','proto'}, use_global_device_ids=true, to_apply=%region_15.16 | all-reduce | flops 1 | bytes 8 | tf_op jit(solution)/shard_map/psum | solution.py:81
  624.6 0.0 reduce-scatter.4.cloned.1.call-done
  624.7 1.7 copy.15
  626.4 2.3 multiply_reduce_fusion.2
  628.7 23.6 %psum.71 = f32[4096]{0:T(1024)S(1)} all-reduce(f32[4096]{0:T(1024)S(1)} %multiply_reduce_fusion.2), channel_id=1, replica_groups=mesh['dp'=8,'proto'=32] {'dp'}, use_global_device_ids=true, to_apply=%region_18.19 | all-reduce | flops 4096 | bytes 32768 | tf_op jit(solution)/shard_map/psum | solution.py:91
  652.3 4.6 subtract_divide_fusion
  656.9 3.1 copy.12
  (36 shorter events, 0.5 us)
Async XLA Ops:
  7.2 36.6 %copy-start = (bf16[768,384]{1,0:T(8,128)(2,1)S(1)}, bf16[768,384]{1,0:T(8,128)(2,1)}, u32[]{:S(2)}) copy-start(bf16[768,384]{1,0:T(8,128)(2,1)} %param.5) | copy-start | bytes 1769476
  7.2 35.4 %copy-start.2 = (bf16[48,4096]{1,0:T(8,128)(2,1)S(1)}, bf16[48,4096]{1,0:T(8,128)(2,1)}, u32[]{:S(2)}) copy-start(bf16[48,4096]{1,0:T(8,128)(2,1)} %param.7) | copy-start | bytes 1179652
  7.2 58.4 %all-gather.2.cloned.1.call-start = ((), (), s32[]{:S(2)}) async-start(), calls=%async_computation.1 | async-start | bytes 3538944 | tf_op jit(solution)/shard_map/all_gather | solution.py:48
  7.2 8.6 %collective-permute-start = (bf16[48,4096]{1,0:T(8,128)(2,1)}, bf16[48,4096]{1,0:T(8,128)(2,1)S(1)}, u32[]{:S(2)}, u32[]{:S(2)}) collective-permute-start(bf16[48,4096]{1,0:T(8,128)(2,1)} %param.7), channel_id=1, source_target_pairs={{0,32},{32,64},{64,96},{96,128},{128,160},{160,192},{192,224},{224... | collective-permute-start | bytes 1179656 | tf_op jit(solution)/shard_map/ppermute | solution.py:27
  15.9 8.4 %collective-permute-start.1 = (bf16[48,4096]{1,0:T(8,128)(2,1)S(1)}, bf16[48,4096]{1,0:T(8,128)(2,1)S(1)}, u32[]{:S(2)}, u32[]{:S(2)}) collective-permute-start(bf16[48,4096]{1,0:T(8,128)(2,1)S(1)} %collective-permute-done), channel_id=1, source_target_pairs={{0,32},{32,64},{64,96},{96,128},{128,160},{160,192},{192,224},{224... | collective-permute-start | bytes 1179656 | tf_op jit(solution)/shard_map/ppermute | solution.py:27
  15.9 8.6 %collective-permute-start.4 = (bf16[48,4096]{1,0:T(8,128)(2,1)}, bf16[48,4096]{1,0:T(8,128)(2,1)S(1)}, u32[]{:S(2)}, u32[]{:S(2)}) collective-permute-start(bf16[48,4096]{1,0:T(8,128)(2,1)} %param.7), channel_id=1, source_target_pairs={{0,224},{32,0},{64,32},{96,64},{128,96},{160,128},{192,160},{224,1... | collective-permute-start | bytes 1179656 | tf_op jit(solution)/shard_map/ppermute | solution.py:31
  24.3 8.4 %collective-permute-start.2 = (bf16[48,4096]{1,0:T(8,128)(2,1)S(1)}, bf16[48,4096]{1,0:T(8,128)(2,1)S(1)}, u32[]{:S(2)}, u32[]{:S(2)}) collective-permute-start(bf16[48,4096]{1,0:T(8,128)(2,1)S(1)} %collective-permute-done.1), channel_id=1, source_target_pairs={{0,32},{32,64},{64,96},{96,128},{128,160},{160,192},{192,224},{224... | collective-permute-start | bytes 1179656 | tf_op jit(solution)/shard_map/ppermute | solution.py:27
  24.4 8.4 %collective-permute-start.5 = (bf16[48,4096]{1,0:T(8,128)(2,1)S(1)}, bf16[48,4096]{1,0:T(8,128)(2,1)S(1)}, u32[]{:S(2)}, u32[]{:S(2)}) collective-permute-start(bf16[48,4096]{1,0:T(8,128)(2,1)S(1)} %collective-permute-done.4), channel_id=1, source_target_pairs={{0,224},{32,0},{64,32},{96,64},{128,96},{160,128},{192,160},{224,1... | collective-permute-start | bytes 1179656 | tf_op jit(solution)/shard_map/ppermute | solution.py:31
  32.7 8.4 %collective-permute-start.3 = (bf16[48,4096]{1,0:T(8,128)(2,1)S(1)}, bf16[48,4096]{1,0:T(8,128)(2,1)S(1)}, u32[]{:S(2)}, u32[]{:S(2)}) collective-permute-start(bf16[48,4096]{1,0:T(8,128)(2,1)S(1)} %collective-permute-done.2), channel_id=1, source_target_pairs={{0,32},{32,64},{64,96},{96,128},{128,160},{160,192},{192,224},{224... | collective-permute-start | bytes 1179656 | tf_op jit(solution)/shard_map/ppermute | solution.py:27
  32.7 591.9 %reduce-scatter.4.cloned.1.call-start = ((), (), s32[]{:S(2)}) async-start(), calls=%async_computation.2 | async-start | bytes 7077888
  32.8 9.5 %collective-permute-start.6 = (bf16[48,4096]{1,0:T(8,128)(2,1)S(1)}, bf16[48,4096]{1,0:T(8,128)(2,1)S(1)}, u32[]{:S(2)}, u32[]{:S(2)}) collective-permute-start(bf16[48,4096]{1,0:T(8,128)(2,1)S(1)} %collective-permute-done.5), channel_id=1, source_target_pairs={{0,224},{32,0},{64,32},{96,64},{128,96},{160,128},{192,160},{224,1... | collective-permute-start | bytes 1179656 | tf_op jit(solution)/shard_map/ppermute | solution.py:31
  43.8 24.4 %copy-start.3 = (bf16[768,384]{1,0:T(8,128)(2,1)S(1)}, bf16[768,384]{1,0:T(8,128)(2,1)}, u32[]{:S(2)}) copy-start(bf16[768,384]{1,0:T(8,128)(2,1)} %param.4) | copy-start | bytes 1769476
  153.1 6.0 copy-start.1
Sparse Core Ops, SparseCore 0:
  32.8 32.7 all-gather.1
  525.9 46.9 reduce-scatter.3
